TPU v7x, 1024 devices: a whole 4x8x16 slice. The times are simulated.
1024 devices in a mesh: tower: 32 (over x_lo, y, core), intra: 32 (over z, x_hi).
Axes of the slice: x: 4 (x_hi: 2, x_lo: 2; x = x_hi * 2 + x_lo), y: 8, z: 16, core: 2. Of those that a mesh axis runs over, the one named last changes fastest.
Arguments:
- ids: int32 [256, 2, 8192], P('tower', None, 'intra'), may hold values from 0 to 511
- arrival: int32 [256, 8192], P('tower', 'intra'), may hold values from 0 to 255, as said below
- tables: bfloat16 [256, 16384, 128], P('tower', 'intra'), may hold values from -6 to 6
- cross_weight: bfloat16 [32, 2, 1024, 1024], P('tower'), may hold values from -0.1875 to 0.1875
- cross_bias: float32 [32, 2, 1024], P('tower'), may hold values from -4 to 4
- compress_weight: bfloat16 [32, 1024, 128], P('tower'), may hold values from -0.1875 to 0.1875
- over_weight: bfloat16 [4096, 512], replicated, may hold values from -0.09375 to 0.09375
- over_bias: float32 [512], replicated, may hold values from -4 to 4
- cotangent: bfloat16 [32, 32, 8, 512], P('intra', 'tower'), may hold values from -6 to 6
Outputs:
- over_out: bfloat16 [32, 32, 8, 512], P('intra', 'tower')
- pooled_grad: bfloat16 [256, 8192, 128], P('tower', 'intra')
Inputs may be any that keep to these rules, and one draw needn't show every extreme that they name: `ids`: row numbers within the table shard that holds the slot. `arrival`: for each feature, every aligned block of 256 positions holds each number 0 to 255 once.
All inputs are finite; a program needn't handle non-finite values.
Results may differ from a plain program's by a relative error of at most 0.018.
Values may be sent and summed in bfloat16 or wider, within the bound.
A program may use at most 32 MiB of HBM per device.

v0:
```python
import jax
import jax.numpy as jnp
from jax import lax
from jax.sharding import PartitionSpec as P


def silu_slope(value):
    sig = jax.nn.sigmoid(value)
    return sig * (1.0 + value * (1.0 - sig))


def local(
    ids,
    arrival,
    tables,
    cross_weight,
    cross_bias,
    compress_weight,
    over_weight,
    over_bias,
    cotangent,
):
    feats = tables.shape[0]
    embed = tables.shape[2]
    width = compress_weight.shape[1]
    samp = ids.shape[2]
    block = cotangent.shape[2]
    weights = cross_weight[0]
    biases = cross_bias[0]
    squeeze = compress_weight[0]
    looked = jax.vmap(lambda tab, idx: jnp.take(tab, idx, axis=0))(tables, ids)
    slot_vals = jnp.sum(looked, axis=1, dtype=jnp.float32).astype(jnp.bfloat16)
    arrived = lax.all_to_all(slot_vals, "intra", split_axis=1, concat_axis=1, tiled=True)
    placed = jax.vmap(lambda a, v: jnp.zeros((samp, embed), jnp.bfloat16).at[a].set(v))(
        arrival, arrived
    )
    first = jnp.transpose(placed, (1, 0, 2)).reshape(samp, width)
    first_f = first.astype(jnp.float32)
    state = first
    zlist = []
    for layer in range(weights.shape[0]):
        zval = (
            jnp.dot(state, weights[layer], preferred_element_type=jnp.float32)
            + biases[layer][None, :]
        )
        zlist.append(zval)
        state = (first_f * zval + state.astype(jnp.float32)).astype(jnp.bfloat16)
    compact = jnp.dot(state, squeeze, preferred_element_type=jnp.float32).astype(jnp.bfloat16)
    incoming = cotangent.reshape(block, cotangent.shape[3]).astype(jnp.float32)
    joined = lax.all_to_all(compact, "tower", split_axis=0, concat_axis=1, tiled=True)
    pre = jnp.dot(joined, over_weight, preferred_element_type=jnp.float32) + over_bias
    dz = (incoming * silu_slope(pre)).astype(jnp.bfloat16)
    d_in = lax.dot_general(
        dz, over_weight, (((1,), (1,)), ((), ())), preferred_element_type=jnp.float32
    ).astype(jnp.bfloat16)
    dcomp = lax.all_to_all(d_in, "tower", split_axis=1, concat_axis=0, tiled=True)
    over_out = jax.nn.silu(pre).astype(jnp.bfloat16).reshape(cotangent.shape)
    grad = lax.dot_general(
        dcomp, squeeze, (((1,), (1,)), ((), ())), preferred_element_type=jnp.float32
    )
    direct = jnp.zeros_like(grad)
    for layer in reversed(range(weights.shape[0])):
        upd = (grad * first_f).astype(jnp.bfloat16)
        direct = direct + grad * zlist[layer]
        grad = grad + lax.dot_general(
            upd, weights[layer], (((1,), (1,)), ((), ())), preferred_element_type=jnp.float32
        )
    final = (grad + direct).astype(jnp.bfloat16).reshape(samp, feats, embed)
    by_feature = jnp.transpose(final, (1, 0, 2))
    leaving = jax.vmap(lambda a, v: jnp.take(v, a, axis=0))(arrival, by_feature)
    pooled_grad = lax.all_to_all(leaving, "intra", split_axis=1, concat_axis=1, tiled=True)
    return (over_out, pooled_grad)


def solution(mesh):
    in_specs = (
        P("tower", None, "intra"),
        P("tower", "intra"),
        P("tower", "intra", None),
        P("tower", None, None, None),
        P("tower", None, None),
        P("tower", None, None),
        P(),
        P(),
        P("intra", "tower", None, None),
    )
    out_specs = (P("intra", "tower", None, None), P("tower", "intra", None))
    return jax.shard_map(local, mesh=mesh, in_specs=in_specs, out_specs=out_specs, check_vma=False)
```

profile of v0, /device:TPU:1, one launch (start us, length us, event | category | flops | bytes accessed | tf_op | source)
XLA Modules:
  0.0 180.4 jit_solution(14041294784451385657)
XLA Ops:
  0.6 0.0 copy-start
  0.6 0.8 fusion.61
  1.5 0.7 compare_and_fusion
  2.2 0.0 copy-done
  2.3 21.7 %gather_fusion = bf16[4096,128]{1,0:T(8,128)(2,1)S(1)} fusion(bf16[8,512,128]{2,1,0:T(8,128)(2,1)S(1)} %copy-done, s32[4096]{0:T(1024)S(1)} %bitcast.109), kind=kCustom, calls=%fused_computation | custom fusion | bytes 2129920 | tf_op jit(solution)/shard_map/vmap(jit(_take))/gather | solution.py:31
  24.0 0.0 copy-start.7
  24.0 0.0 copy-start.11
  24.0 0.0 copy-start.12
  24.0 0.0 copy-start.9
  24.0 0.8 select_reduce_fusion
  24.8 1.1 copy.20
  26.0 22.1 %all-to-all-start = ((bf16[8,256,128]{2,0,1:T(8,128)(2,1)}), bf16[8,256,128]{2,0,1:T(8,128)(2,1)S(1)}, u32[]{:S(2)}, u32[]{:S(2)}) async-start(bf16[8,256,128]{2,0,1:T(8,128)(2,1)} %copy.20), calls=%async_computation | async-start | bytes 1048576 | tf_op jit(solution)/shard_map/all_to_all | solution.py:33
  48.1 0.0 copy-done.7
  48.2 0.0 copy-done.11
  48.2 0.1 multiply_reduce_fusion
  48.2 0.0 copy-done.12
  48.2 0.1 and_reduce_fusion
  48.3 0.0 copy-done.9
  48.4 31.1 %all-to-all-done = bf16[8,256,128]{2,0,1:T(8,128)(2,1)S(1)} async-done(((bf16[8,256,128]{2,0,1:T(8,128)(2,1)}), bf16[8,256,128]{2,0,1:T(8,128)(2,1)S(1)}, u32[]{:S(2)}, u32[]{:S(2)}) %all-to-all-start) | async-done | bytes 524320 | tf_op jit(solution)/shard_map/all_to_all | solution.py:33
  79.5 0.1 copy.21
  79.5 5.9 %scatter_custom_fusion = bf16[2048,128]{1,0:T(8,128)(2,1)S(1)} fusion(s32[2048]{0:T(1024)S(1)} %bitcast.120, bf16[2048,128]{1,0:T(8,128)(2,1)S(1)} %bitcast.119, bf16[]{:T(256)} %constant.21.clone.1), kind=kCustom, calls=%fused_computation.51 | custom fusion | bytes 524290
  85.4 0.0 copy-start.4
  85.4 2.4 %fusion.12 = f32[256,1024]{1,0:T(8,128)S(1)} fusion(bf16[1,2,1024,1024]{3,2,1,0:T(8,128)(2,1)} %param.12, f32[1024]{0:T(1024)S(1)} %bitcast.122, bf16[8,32,8,128]{3,2,1,0:T(8,128)(2,1)S(1)} %bitcast.112), kind=kOutput, calls=%fused_computation.21 | convolution fusion | flops 537133056 | bytes 3674112 | tf_op jit(solution)/shard_map/dot_general | solution.py:43
  87.9 0.4 copy-done.4
  88.2 0.7 fusion.21
  89.0 1.0 copy-done.2
  90.0 1.0 fusion.33
  91.0 9.9 %all-to-all-start.1 = ((bf16[32,8,128]{2,1,0:T(8,128)(2,1)}), bf16[32,8,128]{2,1,0:T(8,128)(2,1)S(1)}, u32[]{:S(2)}, u32[]{:S(2)}) async-start(bf16[32,8,128]{2,1,0:T(8,128)(2,1)} %fusion.33), calls=%async_computation.1 | async-start | bytes 131072 | tf_op jit(solution)/shard_map/all_to_all | solution.py:50
  100.9 0.0 copy-start.8
  100.9 8.0 %all-to-all-done.1 = bf16[32,8,128]{2,1,0:T(8,128)(2,1)S(1)} async-done(((bf16[32,8,128]{2,1,0:T(8,128)(2,1)}), bf16[32,8,128]{2,1,0:T(8,128)(2,1)S(1)}, u32[]{:S(2)}, u32[]{:S(2)}) %all-to-all-start.1) | async-done | bytes 65568 | tf_op jit(solution)/shard_map/all_to_all | solution.py:50
  109.0 3.0 %convolution_add_fusion = f32[8,512]{1,0:T(8,128)S(1)} fusion(bf16[4096,512]{1,0:T(8,128)(2,1)} %param.15, bf16[32,8,128]{2,1,0:T(8,128)(2,1)S(1)} %all-to-all-done.1, f32[512]{0:T(512)S(1)} %copy-done.10), kind=kOutput, calls=%fused_computation.31 | convolution fusion | flops 33558528 | bytes 4278272 | tf_op jit(solution)/shard_map/dot_general | solution.py:51
  112.0 0.5 copy-done.1
  112.4 1.8 %fusion.34 = bf16[8,32,128]{2,0,1:T(8,128)(2,1)} fusion(bf16[4096,512]{1,0:T(8,128)(2,1)S(1)} %copy-done.1, f32[8,512]{1,0:T(8,128)S(1)} %convolution_add_fusion, bf16[1,1,8,512]{3,2,1,0:T(8,128)(2,1)S(1)} %copy-done.8), kind=kOutput, calls=%fused_computation.30 | convolution fusion | flops 33628160 | bytes 4284416 | tf_op jit(solution)/shard_map/dot_general | solution.py:53
  114.2 4.7 %all-to-all-start.2 = ((bf16[8,32,128]{2,0,1:T(8,128)(2,1)}), bf16[8,32,128]{2,0,1:T(8,128)(2,1)S(1)}, u32[]{:S(2)}, u32[]{:S(2)}) async-start(bf16[8,32,128]{2,0,1:T(8,128)(2,1)} %fusion.34), calls=%async_computation.2 | async-start | bytes 131072 | tf_op jit(solution)/shard_map/all_to_all | solution.py:56
  119.0 0.2 copy.23
  119.2 8.0 %all-to-all-done.2 = bf16[8,32,128]{2,0,1:T(8,128)(2,1)S(1)} async-done(((bf16[8,32,128]{2,0,1:T(8,128)(2,1)}), bf16[8,32,128]{2,0,1:T(8,128)(2,1)S(1)}, u32[]{:S(2)}, u32[]{:S(2)}) %all-to-all-start.2) | async-done | bytes 65568 | tf_op jit(solution)/shard_map/all_to_all | solution.py:56
  127.1 0.3 fusion.51
  127.5 2.5 %fusion.24 = f32[256,1024]{1,0:T(8,128)S(1)} fusion(f32[256,1024]{1,0:T(8,128)S(1)} %fusion.51, bf16[1,2,1024,1024]{3,2,1,0:T(8,128)(2,1)} %param.12, bf16[8,32,8,128]{3,2,1,0:T(8,128)(2,1)S(1)} %bitcast.115), kind=kOutput, calls=%fused_computation.25 | convolution fusion | flops 537919488 | bytes 5767168 | tf_op jit(solution)/shard_map/dot_general | solution.py:65
  130.0 0.0 copy-done.5
  130.0 0.3 copy-done.3
  130.3 1.0 fusion.30
  131.3 0.1 copy.55
  131.4 11.1 %gather_fusion.1 = bf16[2048,128]{1,0:T(8,128)(2,1)S(1)} fusion(bf16[8,256,128]{2,1,0:T(8,128)(2,1)S(1)} %bitcast.111, s32[2048]{0:T(1024)S(1)} %bitcast.110), kind=kCustom, calls=%fused_computation.1 | custom fusion | bytes 1064960 | tf_op jit(solution)/shard_map/vmap(jit(_take))/gather | solution.py:70
  142.6 1.2 copy_select_fusion
  143.8 5.2 %all-to-all-start.3 = ((bf16[8,256,128]{2,0,1:T(8,128)(2,1)}), bf16[8,256,128]{2,0,1:T(8,128)(2,1)S(1)}, u32[]{:S(2)}, u32[]{:S(2)}) async-start(bf16[8,256,128]{2,0,1:T(8,128)(2,1)} %copy_select_fusion), calls=%async_computation.3 | async-start | bytes 1048576 | tf_op jit(solution)/shard_map/all_to_all | solution.py:71
  149.0 0.6 fusion.65
  149.6 29.9 %all-to-all-done.3 = bf16[8,256,128]{2,0,1:T(8,128)(2,1)S(1)} async-done(((bf16[8,256,128]{2,0,1:T(8,128)(2,1)}), bf16[8,256,128]{2,0,1:T(8,128)(2,1)S(1)}, u32[]{:S(2)}, u32[]{:S(2)}) %all-to-all-start.3) | async-done | bytes 524320 | tf_op jit(solution)/shard_map/all_to_all | solution.py:71
  179.5 0.9 copy.26
  (18 shorter events, 0.1 us)
Async XLA Ops:
  0.6 1.6 copy-start
  24.0 24.2 %copy-start.7 = (s32[8,256]{1,0:T(8,128)S(1)}, s32[8,256]{1,0:T(8,128)}, u32[]{:S(2)}) copy-start(s32[8,256]{1,0:T(8,128)} %param.10) | copy-start | bytes 24580
  24.0 24.2 %copy-start.11 = (s32[2]{0:T(128)S(1)}, s32[2]{0:T(128)}, u32[]{:S(2)}) copy-start(s32[2]{0:T(128)} %constant.47) | copy-start | bytes 28
  24.0 24.3 %copy-start.12 = (s32[2]{0:T(128)S(1)}, s32[2]{0:T(128)}, u32[]{:S(2)}) copy-start(s32[2]{0:T(128)} %constant.50) | copy-start | bytes 28
  24.0 24.3 %copy-start.9 = (f32[1,2,1024]{2,1,0:T(2,128)S(1)}, f32[1,2,1024]{2,1,0:T(2,128)}, u32[]{:S(2)}) copy-start(f32[1,2,1024]{2,1,0:T(2,128)} %param.13) | copy-start | bytes 24580
  26.0 53.5 %all-to-all-start = ((bf16[8,256,128]{2,0,1:T(8,128)(2,1)}), bf16[8,256,128]{2,0,1:T(8,128)(2,1)S(1)}, u32[]{:S(2)}, u32[]{:S(2)}) async-start(bf16[8,256,128]{2,0,1:T(8,128)(2,1)} %copy.20), calls=%async_computation | async-start | bytes 1048576 | tf_op jit(solution)/shard_map/all_to_all | solution.py:33
  85.4 2.8 %copy-start.4 = (bf16[1,2,1024,1024]{3,2,1,0:T(8,128)(2,1)S(1)}, bf16[1,2,1024,1024]{3,2,1,0:T(8,128)(2,1)}, u32[]{:S(2)}) copy-start(bf16[1,2,1024,1024]{3,2,1,0:T(8,128)(2,1)} %param.12) | copy-start | bytes 12582916
  88.2 1.7 copy-start.6
  89.0 1.0 copy-start.2
  90.0 19.0 %copy-start.10 = (f32[512]{0:T(512)S(1)}, f32[512]{0:T(512)}, u32[]{:S(2)}) copy-start(f32[512]{0:T(512)} %param.16) | copy-start | bytes 6148
  91.0 18.0 %all-to-all-start.1 = ((bf16[32,8,128]{2,1,0:T(8,128)(2,1)}), bf16[32,8,128]{2,1,0:T(8,128)(2,1)S(1)}, u32[]{:S(2)}, u32[]{:S(2)}) async-start(bf16[32,8,128]{2,1,0:T(8,128)(2,1)} %fusion.33), calls=%async_computation.1 | async-start | bytes 131072 | tf_op jit(solution)/shard_map/all_to_all | solution.py:50
  100.9 11.0 %copy-start.8 = (bf16[1,1,8,512]{3,2,1,0:T(8,128)(2,1)S(1)}, bf16[1,1,8,512]{3,2,1,0:T(8,128)(2,1)}, u32[]{:S(2)}) copy-start(bf16[1,1,8,512]{3,2,1,0:T(8,128)(2,1)} %param.17) | copy-start | bytes 24580
  109.0 3.5 %copy-start.1 = (bf16[4096,512]{1,0:T(8,128)(2,1)S(1)}, bf16[4096,512]{1,0:T(8,128)(2,1)}, u32[]{:S(2)}) copy-start(bf16[4096,512]{1,0:T(8,128)(2,1)} %param.15) | copy-start | bytes 12582916
  114.2 12.9 %all-to-all-start.2 = ((bf16[8,32,128]{2,0,1:T(8,128)(2,1)}), bf16[8,32,128]{2,0,1:T(8,128)(2,1)S(1)}, u32[]{:S(2)}, u32[]{:S(2)}) async-start(bf16[8,32,128]{2,0,1:T(8,128)(2,1)} %fusion.34), calls=%async_computation.2 | async-start | bytes 131072 | tf_op jit(solution)/shard_map/all_to_all | solution.py:56
  127.1 2.9 %copy-start.5 = (bf16[1,2,1024,1024]{3,2,1,0:T(8,128)(2,1)S(1)}, bf16[1,2,1024,1024]{3,2,1,0:T(8,128)(2,1)}, u32[]{:S(2)}) copy-start(bf16[1,2,1024,1024]{3,2,1,0:T(8,128)(2,1)} %param.12) | copy-start | bytes 12582916
  127.4 2.9 %copy-start.3 = (f32[256,1024]{1,0:T(8,128)S(1)}, f32[256,1024]{1,0:T(8,128)}, u32[]{:S(2)}) copy-start(f32[256,1024]{1,0:T(8,128)} %copy-done.2) | copy-start | bytes 3145732
  143.8 35.7 %all-to-all-start.3 = ((bf16[8,256,128]{2,0,1:T(8,128)(2,1)}), bf16[8,256,128]{2,0,1:T(8,128)(2,1)S(1)}, u32[]{:S(2)}, u32[]{:S(2)}) async-start(bf16[8,256,128]{2,0,1:T(8,128)(2,1)} %copy_select_fusion), calls=%async_computation.3 | async-start | bytes 1048576 | tf_op jit(solution)/shard_map/all_to_all | solution.py:71
where the time goes:
time: 183 us; the launch traced here: 180 us
  waiting for transfers between devices  77 us (42%)
  local copies, waits for them, and re-layouts  43.2 us (24%)
  starting transfers between devices  42 us (23%)
  matrix products  12.8 us (7%)
  other arithmetic  4.4 us (2%)
    all_to_all x1, waiting for transfers between devices, local(): lax.all_to_all(slot_vals, 'intra', split_axis=1, concat_axis=1, tiled=True)  31.1 us
    all_to_all x1, waiting for transfers between devices, local(): lax.all_to_all(leaving, 'intra', split_axis=1, concat_axis=1, tiled=True)  29.9 us
    all_to_all x1, starting transfers between devices, local(): lax.all_to_all(slot_vals, 'intra', split_axis=1, concat_axis=1, tiled=True)  22.1 us
    gather x1, local copies, waits for them, and re-layouts, local(): looked = jax.vmap(lambda tab, idx: jnp.take(tab, idx, axis=0))(tables, ids)  21.7 us
    gather x1, local copies, waits for them, and re-layouts, local(): leaving = jax.vmap(lambda a, v: jnp.take(v, a, axis=0))(arrival, by_feature)  11.1 us
    all_to_all x1, starting transfers between devices, local(): lax.all_to_all(compact, 'tower', split_axis=0, concat_axis=1, tiled=True)  9.91 us
    unnamed x31, local copies, waits for them, and re-layouts  8.94 us
    all_to_all x1, waiting for transfers between devices, local(): lax.all_to_all(compact, 'tower', split_axis=0, concat_axis=1, tiled=True)  8.03 us
  transfers between devices with their start and end apart: 4, of which 4 were waited for; matrix products, arithmetic and copies ran while one was open for 1% of the time, Pallas kernels for 0%

commit v1 on v0

v1 whole, which is shorter than its diff:
```python
import functools

import jax
import jax.numpy as jnp
from jax import lax
from jax.experimental import pallas as pl
from jax.experimental.pallas import tpu as pltpu
from jax.sharding import PartitionSpec as P

MESH = pl.DeviceIdType.MESH
F32 = jnp.float32
BF16 = jnp.bfloat16
NT_DIMS = (((1,), (1,)), ((), ()))


def dot(a, b):
    return jnp.dot(a, b, preferred_element_type=F32)


def dot_t(a, b):
    return lax.dot_general(a, b, NT_DIMS, preferred_element_type=F32)


def kernel(
    ni,
    nt,
    ids_hbm,
    arr_hbm,
    tab_hbm,
    cw_hbm,
    cb_hbm,
    sq_hbm,
    ow_hbm,
    ob_hbm,
    ct_hbm,
    out_ref,
    grad_ref,
    ids_ref,
    arr_ref,
    tab_ref,
    cw_ref,
    cb_ref,
    sq_ref,
    ow_ref,
    ob_ref,
    ct_ref,
    send1,
    recv1,
    csend,
    joined,
    dsend,
    dcomp,
    send2,
    perm,
    perm_t,
    first,
    state1,
    state2,
    zbuf,
    gbuf,
    direct,
    upd,
    final,
    in_sem,
    own_sem,
    send_sem,
    recv_sem,
):
    feats, rows, embed = tab_ref.shape
    samp = arr_ref.shape[1]
    width = cw_ref.shape[2]
    block = samp // ni
    half = ni // 2
    tile = min(256, width)
    tiles = width // tile
    me_i = lax.axis_index("intra")
    me_t = lax.axis_index("tower")

    barrier = pltpu.get_barrier_semaphore()

    def greet_i(step, carry):
        peer = lax.rem(me_i + step, ni)
        pl.semaphore_signal(barrier, inc=1, device_id={"intra": peer}, device_id_type=MESH)
        return carry

    def greet_t(step, carry):
        peer = lax.rem(me_t + step, nt)
        pl.semaphore_signal(barrier, inc=1, device_id={"tower": peer}, device_id_type=MESH)
        return carry

    lax.fori_loop(1, ni, greet_i, 0)
    lax.fori_loop(1, nt, greet_t, 0)

    loads = [
        pltpu.make_async_copy(src, dst, in_sem.at[at])
        for at, (src, dst) in enumerate(
            (
                (ids_hbm, ids_ref),
                (arr_hbm, arr_ref),
                (tab_hbm, tab_ref),
                (cw_hbm.at[0], cw_ref),
                (cb_hbm.at[0], cb_ref),
                (sq_hbm.at[0], sq_ref),
                (ow_hbm, ow_ref),
                (ob_hbm, ob_ref),
                (ct_hbm.at[0, 0], ct_ref),
            )
        )
    ]
    for load in loads:
        load.start()
    loads[0].wait()
    loads[1].wait()

    ids = ids_ref[...].reshape(feats * 2, samp)
    arr = arr_ref[...]
    pad = jnp.zeros((128 - 3 * feats, samp), jnp.int32)
    columns = jnp.concatenate([ids, arr, pad], axis=0).T

    loads[2].wait()
    row_id = lax.broadcasted_iota(jnp.int32, (samp, rows), 1)
    for f in range(feats):
        hot = jnp.where(columns[:, 2 * f : 2 * f + 1] == row_id, 1.0, 0.0)
        hot = hot + jnp.where(columns[:, 2 * f + 1 : 2 * f + 2] == row_id, 1.0, 0.0)
        pooled = dot(hot.astype(BF16), tab_ref[f])
        send1[:, f] = pooled.reshape(ni, block, embed).astype(BF16)

    pl.semaphore_wait(barrier, ni + nt - 2)

    def peer_of(step):
        k = step // 2
        near = half // 2 - (k + 1) // 2
        far = half // 2 + k // 2
        dz = jnp.where(lax.rem(k, 2) == 1, near, far)
        z = lax.rem(me_i // 2 + dz, half)
        xh = lax.rem(lax.rem(me_i, 2) + 1 - lax.rem(step, 2), 2)
        return z * 2 + xh

    def exchange(src, dst, send, recv, axis, count, me, dst_at):
        def start(step, carry):
            if axis == "intra":
                peer = peer_of(step)
            else:
                peer = lax.rem(me + step + 1, count)
            pltpu.make_async_remote_copy(
                src_ref=src(peer),
                dst_ref=dst(me),
                send_sem=send,
                recv_sem=recv,
                device_id={axis: peer},
                device_id_type=MESH,
            ).start()
            return carry

        lax.fori_loop(0, count - 1, start, 0)
        own = pltpu.make_async_copy(src(me), dst(me), own_sem.at[dst_at])
        own.start()
        return own

    own1 = exchange(
        lambda p: send1.at[p], lambda p: recv1.at[p], send_sem.at[0], recv_sem.at[0], "intra", ni, me_i, 0
    )

    s_row = lax.broadcasted_iota(jnp.int32, (samp, samp), 0)
    s_col = lax.broadcasted_iota(jnp.int32, (samp, samp), 1)
    for f in range(feats):
        perm[f] = jnp.where(arr[f : f + 1, :] == s_row, 1.0, 0.0).astype(BF16)
        at = 2 * feats + f
        perm_t[f] = jnp.where(columns[:, at : at + 1] == s_col, 1.0, 0.0).astype(BF16)
    for load in loads[3:]:
        load.wait()

    def all_but_one(ref, sem, count):
        pltpu.make_async_copy(ref.at[pl.ds(0, count - 1)], ref.at[pl.ds(0, count - 1)], sem).wait()

    own1.wait()
    all_but_one(recv1, recv_sem.at[0], ni)

    for f in range(feats):
        got = recv1[:, f].astype(F32).reshape(samp, embed).astype(BF16)
        first[:, f * embed : (f + 1) * embed] = dot(perm[f], got).astype(BF16)

    def forward(layer, src, dst):
        def step(n, carry):
            cols = pl.ds(pl.multiple_of(n * tile, tile), tile)
            zval = dot(src[...], cw_ref[layer, :, cols]) + cb_ref[pl.ds(layer, 1), cols]
            zbuf[layer, :, cols] = zval
            dst[:, cols] = (first[:, cols].astype(F32) * zval + src[:, cols].astype(F32)).astype(BF16)
            return carry

        lax.fori_loop(0, tiles, step, 0)

    forward(0, first, state1)
    forward(1, state1, state2)
    csend[...] = dot(state2[...], sq_ref[...]).reshape(nt, samp // nt, -1).astype(BF16)

    own2 = exchange(
        lambda p: csend.at[p], lambda p: joined.at[p], send_sem.at[1], recv_sem.at[1], "tower", nt, me_t, 1
    )
    own2.wait()
    all_but_one(joined, recv_sem.at[1], nt)

    comp = joined.shape[2]
    whole = jnp.concatenate([joined[t] for t in range(nt)], axis=1)
    pre = dot(whole, ow_ref[...]) + ob_ref[...]
    sig = jax.nn.sigmoid(pre)
    out_ref[0, 0] = (pre * sig).astype(BF16)
    dz = (ct_ref[...].astype(F32) * (sig * (1.0 + pre * (1.0 - sig)))).astype(BF16)
    d_in = dot_t(dz, ow_ref[...]).astype(BF16)
    for t in range(nt):
        dsend[t] = d_in[:, t * comp : (t + 1) * comp]

    own3 = exchange(
        lambda p: dsend.at[p], lambda p: dcomp.at[p], send_sem.at[2], recv_sem.at[2], "tower", nt, me_t, 2
    )
    own3.wait()
    all_but_one(dcomp, recv_sem.at[2], nt)

    dc = dcomp[...].astype(F32).reshape(samp, comp).astype(BF16)

    def back_top(n, carry):
        cols = pl.ds(pl.multiple_of(n * tile, tile), tile)
        grad = dot_t(dc, sq_ref[cols, :])
        gbuf[:, cols] = grad
        direct[:, cols] = grad * zbuf[1, :, cols]
        upd[1, :, cols] = (grad * first[:, cols].astype(F32)).astype(BF16)
        return carry

    def back_one(n, carry):
        cols = pl.ds(pl.multiple_of(n * tile, tile), tile)
        grad = gbuf[:, cols] + dot_t(upd[1], cw_ref[1, cols, :])
        gbuf[:, cols] = grad
        direct[:, cols] += grad * zbuf[0, :, cols]
        upd[0, :, cols] = (grad * first[:, cols].astype(F32)).astype(BF16)
        return carry

    def back_zero(n, carry):
        cols = pl.ds(pl.multiple_of(n * tile, tile), tile)
        grad = gbuf[:, cols] + dot_t(upd[0], cw_ref[0, cols, :])
        final[:, cols] = (grad + direct[:, cols]).astype(BF16)
        return carry

    lax.fori_loop(0, tiles, back_top, 0)
    lax.fori_loop(0, tiles, back_one, 0)
    lax.fori_loop(0, tiles, back_zero, 0)
    for f in range(feats):
        leaving = dot(perm_t[f], final[:, f * embed : (f + 1) * embed])
        send2[:, f] = leaving.reshape(ni, block, embed).astype(BF16)

    own4 = exchange(
        lambda p: send2.at[p], lambda p: grad_ref.at[:, p], send_sem.at[3], recv_sem.at[3], "intra", ni, me_i, 3
    )
    own4.wait()
    pltpu.make_async_copy(
        grad_ref.at[:, pl.ds(0, ni - 1)], grad_ref.at[:, pl.ds(0, ni - 1)], recv_sem.at[3]
    ).wait()
    all_but_one(send1, send_sem.at[0], ni)
    all_but_one(csend, send_sem.at[1], nt)
    all_but_one(dsend, send_sem.at[2], nt)
    all_but_one(send2, send_sem.at[3], ni)


def local(ids, arrival, tables, cross_weight, cross_bias, squeeze, over_weight, over_bias, cotangent, ni, nt):
    feats, rows, embed = tables.shape
    samp = arrival.shape[1]
    width = cross_weight.shape[2]
    comp = squeeze.shape[2]
    wide = over_weight.shape[1]
    rblock = cotangent.shape[2]
    block = samp // ni
    any_spec = pl.BlockSpec(memory_space=pl.ANY)
    vmem_spec = pl.BlockSpec(memory_space=pltpu.VMEM)
    over_out, grad = pl.pallas_call(
        functools.partial(kernel, ni, nt),
        out_shape=(
            jax.ShapeDtypeStruct(cotangent.shape, BF16),
            jax.ShapeDtypeStruct((feats, ni, block, embed), BF16),
        ),
        in_specs=[any_spec] * 9,
        out_specs=(vmem_spec, vmem_spec),
        scratch_shapes=[
            pltpu.VMEM((feats, 2, samp), jnp.int32),
            pltpu.VMEM((feats, samp), jnp.int32),
            pltpu.VMEM((feats, rows, embed), BF16),
            pltpu.VMEM((2, width, width), BF16),
            pltpu.VMEM((2, width), F32),
            pltpu.VMEM((width, comp), BF16),
            pltpu.VMEM((nt * comp, wide), BF16),
            pltpu.VMEM((1, wide), F32),
            pltpu.VMEM((rblock, wide), BF16),
            pltpu.VMEM((ni, feats, block, embed), BF16),
            pltpu.VMEM((ni, feats, block, embed), BF16),
            pltpu.VMEM((nt, rblock, comp), BF16),
            pltpu.VMEM((nt, rblock, comp), BF16),
            pltpu.VMEM((nt, rblock, comp), BF16),
            pltpu.VMEM((nt, rblock, comp), BF16),
            pltpu.VMEM((ni, feats, block, embed), BF16),
            pltpu.VMEM((feats, samp, samp), BF16),
            pltpu.VMEM((feats, samp, samp), BF16),
            pltpu.VMEM((samp, width), BF16),
            pltpu.VMEM((samp, width), BF16),
            pltpu.VMEM((samp, width), BF16),
            pltpu.VMEM((2, samp, width), F32),
            pltpu.VMEM((samp, width), F32),
            pltpu.VMEM((samp, width), F32),
            pltpu.VMEM((2, samp, width), BF16),
            pltpu.VMEM((samp, width), BF16),
            pltpu.SemaphoreType.DMA((9,)),
            pltpu.SemaphoreType.DMA((4,)),
            pltpu.SemaphoreType.DMA((4,)),
            pltpu.SemaphoreType.DMA((4,)),
        ],
        compiler_params=pltpu.CompilerParams(
            collective_id=0, has_side_effects=True, vmem_limit_bytes=60 * 1024 * 1024
        ),
    )(ids, arrival, tables, cross_weight, cross_bias, squeeze, over_weight, over_bias[None, :], cotangent)
    return over_out, grad.reshape(feats, samp, embed)


def solution(mesh):
    in_specs = (
        P("tower", None, "intra"),
        P("tower", "intra"),
        P("tower", "intra", None),
        P("tower", None, None, None),
        P("tower", None, None),
        P("tower", None, None),
        P(),
        P(),
        P("intra", "tower", None, None),
    )
    out_specs = (P("intra", "tower", None, None), P("tower", "intra", None))
    body = functools.partial(local, ni=mesh.shape["intra"], nt=mesh.shape["tower"])
    return jax.shard_map(body, mesh=mesh, in_specs=in_specs, out_specs=out_specs, check_vma=False)
```

time: 183 us -> 99.7 us (0.54); the launches traced: 180 us -> 99.5 us
  Pallas kernels: 0 us -> 95.6 us
  waiting for transfers between devices: 77 us -> 0 us
  starting transfers between devices: 42 us -> 0 us
  local copies, waits for them, and re-layouts: 43.2 us -> 3.17 us
  matrix products: 12.8 us -> 0 us
  other arithmetic: 4.4 us -> 0 us
    pallas_call x0 -> x1, Pallas kernels: none -> 95.6 us  [local(): pl.pallas_call(functools.partial(kernel, ni, nt), out_shape=(jax.ShapeDty...]
    all_to_all x4 -> x0, waiting for transfers between devices: 77 us -> none  [the longest x1 31.1 us: local(): lax.all_to_all(slot_vals, 'intra', split_axis=1, concat_axis=1, tiled=True)]
    all_to_all x4 -> x0, starting transfers between devices: 42 us -> none  [the longest x1 22.1 us: local(): lax.all_to_all(slot_vals, 'intra', split_axis=1, concat_axis=1, tiled=True)]
    gather x2 -> x0, local copies, waits for them, and re-layouts: 32.8 us -> none  [the longest x1 21.7 us: local(): looked = jax.vmap(lambda tab, idx: jnp.take(tab, idx, axis=0))(tables, ids)]
    dot_general x8 -> x0, matrix products: 12.8 us -> none  [the longest x2 3.53 us: local(): lax.dot_general(upd, weights[layer], (((1,), (1,)), ((), ())), preferred_...]
    unnamed x31 -> x2, local copies, waits for them, and re-layouts: 8.94 us -> 3.17 us
  transfers between devices with their start and end apart: 4 -> 0, of which waited for: 4 -> 0; matrix products, arithmetic and copies ran while one was open for 1% -> 0% of each run, Pallas kernels for 0% -> 0%
where the time goes in v1:
time: 99.7 us; the launch traced here: 99.5 us
  Pallas kernels  95.6 us (96%)
  local copies, waits for them, and re-layouts  3.17 us (3%)
    pallas_call x1, Pallas kernels, local(): pl.pallas_call(functools.partial(kernel, ni, nt), out_shape=(jax.ShapeDty...  95.6 us
    unnamed x2, local copies, waits for them, and re-layouts  3.17 us

profile of v1, /device:TPU:1, one launch (start us, length us, event | category | flops | bytes accessed | tf_op | source)
XLA Modules:
  0.0 99.5 jit_solution(7254488679181740942)
XLA Ops:
  0.6 95.6 %shard_map.104 = (bf16[1,1,8,512]{3,2,1,0:T(8,128)(2,1)}, bf16[8,32,8,128]{3,2,1,0:T(8,128)(2,1)}) custom-call(s32[8,2,256]{2,1,0:T(2,128)} %ids_hbm.1, s32[8,256]{1,0:T(8,128)} %arr_hbm.1, bf16[8,512,128]{2,1,0:T(8,128)(2,1)} %tab_hbm.1, bf16[1,2,1024,1024]{3,2,1,0:T(8,128)(2,1)} %cw_hbm.1, f32[1,2,1024]{2,1,0:T(2,128)} %cb_hbm.1, ...), custom_call_target="tpu_custom_call" | custom-call | tf_op jit(solution)/shard_map/pallas_call | solution.py:273
  96.3 1.3 %copy.13 = bf16[1,1,8,512]{3,2,1,0:T(8,128)(2,1)} copy(bf16[1,1,8,512]{3,2,1,0:T(8,128)(2,1)} %get-tuple-element.8) | data formatting | bytes 16384
  97.6 1.9 %copy.14 = bf16[8,256,128]{2,1,0:T(8,128)(2,1)} copy(bf16[8,256,128]{2,1,0:T(8,128)(2,1)} %bitcast.2) | data formatting | bytes 1048576

commit v2 on v1

--- a/solution.py
+++ b/solution.py
@@ -24,6 +24,7 @@
 def kernel(
     ni,
     nt,
+    groups,
     ids_hbm,
     arr_hbm,
     tab_hbm,
@@ -78,8 +79,18 @@
 
     barrier = pltpu.get_barrier_semaphore()
 
+    def peer_of(step, sets):
+        each = half // sets
+        k = lax.rem(step // 2, each)
+        near = -((k + 1) // 2)
+        shift = jnp.where(lax.rem(k, 2) == 1, near, k // 2) + each // 2
+        base = lax.rem((step // 2) // each + half - me_i // 2, sets)
+        z = lax.rem(me_i // 2 + base + sets * shift, half)
+        xh = lax.rem(lax.rem(me_i, 2) + 1 - lax.rem(step, 2), 2)
+        return z * 2 + xh
+
     def greet_i(step, carry):
-        peer = lax.rem(me_i + step, ni)
+        peer = peer_of(step, 1)
         pl.semaphore_signal(barrier, inc=1, device_id={"intra": peer}, device_id_type=MESH)
         return carry
 
@@ -88,7 +99,7 @@
         pl.semaphore_signal(barrier, inc=1, device_id={"tower": peer}, device_id_type=MESH)
         return carry
 
-    lax.fori_loop(1, ni, greet_i, 0)
+    lax.fori_loop(0, ni - 1, greet_i, 0)
     lax.fori_loop(1, nt, greet_t, 0)
 
     loads = [
@@ -127,39 +138,49 @@
 
     pl.semaphore_wait(barrier, ni + nt - 2)
 
-    def peer_of(step):
-        k = step // 2
-        near = half // 2 - (k + 1) // 2
-        far = half // 2 + k // 2
-        dz = jnp.where(lax.rem(k, 2) == 1, near, far)
-        z = lax.rem(me_i // 2 + dz, half)
-        xh = lax.rem(lax.rem(me_i, 2) + 1 - lax.rem(step, 2), 2)
-        return z * 2 + xh
-
-    def exchange(src, dst, send, recv, axis, count, me, dst_at):
+    def exchange_i(src, dst, at, sets):
+        own = pltpu.make_async_copy(src(me_i), dst(me_i), own_sem.at[at])
+        own.start()
+
         def start(step, carry):
-            if axis == "intra":
-                peer = peer_of(step)
-            else:
-                peer = lax.rem(me + step + 1, count)
+            peer = peer_of(step, sets)
+
+            @pl.when(peer != me_i)
+            def _():
+                pltpu.make_async_remote_copy(
+                    src_ref=src(peer),
+                    dst_ref=dst(me_i),
+                    send_sem=send_sem.at[at],
+                    recv_sem=recv_sem.at[at],
+                    device_id={"intra": peer},
+                    device_id_type=MESH,
+                ).start()
+
+            return carry
+
+        lax.fori_loop(0, ni, start, 0)
+        return own
+
+    def exchange_t(src, dst, at):
+        own = pltpu.make_async_copy(src(me_t), dst(me_t), own_sem.at[at])
+        own.start()
+
+        def start(step, carry):
+            peer = lax.rem(me_t + step, nt)
             pltpu.make_async_remote_copy(
                 src_ref=src(peer),
-                dst_ref=dst(me),
-                send_sem=send,
-                recv_sem=recv,
-                device_id={axis: peer},
+                dst_ref=dst(me_t),
+                send_sem=send_sem.at[at],
+                recv_sem=recv_sem.at[at],
+                device_id={"tower": peer},
                 device_id_type=MESH,
             ).start()
             return carry
 
-        lax.fori_loop(0, count - 1, start, 0)
-        own = pltpu.make_async_copy(src(me), dst(me), own_sem.at[dst_at])
-        own.start()
+        lax.fori_loop(1, nt, start, 0)
         return own
 
-    own1 = exchange(
-        lambda p: send1.at[p], lambda p: recv1.at[p], send_sem.at[0], recv_sem.at[0], "intra", ni, me_i, 0
-    )
+    own1 = exchange_i(lambda p: send1.at[p], lambda p: recv1.at[p], 0, groups)
 
     s_row = lax.broadcasted_iota(jnp.int32, (samp, samp), 0)
     s_col = lax.broadcasted_iota(jnp.int32, (samp, samp), 1)
@@ -181,22 +202,17 @@
         first[:, f * embed : (f + 1) * embed] = dot(perm[f], got).astype(BF16)
 
     def forward(layer, src, dst):
-        def step(n, carry):
-            cols = pl.ds(pl.multiple_of(n * tile, tile), tile)
-            zval = dot(src[...], cw_ref[layer, :, cols]) + cb_ref[pl.ds(layer, 1), cols]
+        for n in range(tiles):
+            cols = slice(n * tile, (n + 1) * tile)
+            zval = dot(src[...], cw_ref[layer, :, cols]) + cb_ref[layer : layer + 1, cols]
             zbuf[layer, :, cols] = zval
             dst[:, cols] = (first[:, cols].astype(F32) * zval + src[:, cols].astype(F32)).astype(BF16)
-            return carry
-
-        lax.fori_loop(0, tiles, step, 0)
 
     forward(0, first, state1)
     forward(1, state1, state2)
     csend[...] = dot(state2[...], sq_ref[...]).reshape(nt, samp // nt, -1).astype(BF16)
 
-    own2 = exchange(
-        lambda p: csend.at[p], lambda p: joined.at[p], send_sem.at[1], recv_sem.at[1], "tower", nt, me_t, 1
-    )
+    own2 = exchange_t(lambda p: csend.at[p], lambda p: joined.at[p], 1)
     own2.wait()
     all_but_one(joined, recv_sem.at[1], nt)
 
@@ -210,46 +226,42 @@
     for t in range(nt):
         dsend[t] = d_in[:, t * comp : (t + 1) * comp]
 
-    own3 = exchange(
-        lambda p: dsend.at[p], lambda p: dcomp.at[p], send_sem.at[2], recv_sem.at[2], "tower", nt, me_t, 2
-    )
+    own3 = exchange_t(lambda p: dsend.at[p], lambda p: dcomp.at[p], 2)
     own3.wait()
     all_but_one(dcomp, recv_sem.at[2], nt)
 
     dc = dcomp[...].astype(F32).reshape(samp, comp).astype(BF16)
 
-    def back_top(n, carry):
-        cols = pl.ds(pl.multiple_of(n * tile, tile), tile)
+    def back_top(n):
+        cols = slice(n * tile, (n + 1) * tile)
         grad = dot_t(dc, sq_ref[cols, :])
         gbuf[:, cols] = grad
         direct[:, cols] = grad * zbuf[1, :, cols]
         upd[1, :, cols] = (grad * first[:, cols].astype(F32)).astype(BF16)
-        return carry
-
-    def back_one(n, carry):
-        cols = pl.ds(pl.multiple_of(n * tile, tile), tile)
+
+    def back_one(n):
+        cols = slice(n * tile, (n + 1) * tile)
         grad = gbuf[:, cols] + dot_t(upd[1], cw_ref[1, cols, :])
         gbuf[:, cols] = grad
         direct[:, cols] += grad * zbuf[0, :, cols]
         upd[0, :, cols] = (grad * first[:, cols].astype(F32)).astype(BF16)
-        return carry
-
-    def back_zero(n, carry):
-        cols = pl.ds(pl.multiple_of(n * tile, tile), tile)
+
+    def back_zero(n):
+        cols = slice(n * tile, (n + 1) * tile)
         grad = gbuf[:, cols] + dot_t(upd[0], cw_ref[0, cols, :])
         final[:, cols] = (grad + direct[:, cols]).astype(BF16)
-        return carry
-
-    lax.fori_loop(0, tiles, back_top, 0)
-    lax.fori_loop(0, tiles, back_one, 0)
-    lax.fori_loop(0, tiles, back_zero, 0)
+
+    for n in range(tiles):
+        back_top(n)
+    for n in range(tiles):
+        back_one(n)
+    for n in range(tiles):
+        back_zero(n)
     for f in range(feats):
         leaving = dot(perm_t[f], final[:, f * embed : (f + 1) * embed])
         send2[:, f] = leaving.reshape(ni, block, embed).astype(BF16)
 
-    own4 = exchange(
-        lambda p: send2.at[p], lambda p: grad_ref.at[:, p], send_sem.at[3], recv_sem.at[3], "intra", ni, me_i, 3
-    )
+    own4 = exchange_i(lambda p: send2.at[p], lambda p: grad_ref.at[:, p], 3, 1)
     own4.wait()
     pltpu.make_async_copy(
         grad_ref.at[:, pl.ds(0, ni - 1)], grad_ref.at[:, pl.ds(0, ni - 1)], recv_sem.at[3]
@@ -260,7 +272,7 @@
     all_but_one(send2, send_sem.at[3], ni)
 
 
-def local(ids, arrival, tables, cross_weight, cross_bias, squeeze, over_weight, over_bias, cotangent, ni, nt):
+def local(ids, arrival, tables, cross_weight, cross_bias, squeeze, over_weight, over_bias, cotangent, ni, nt, groups=4, cid=0, name=None, vmem=32):
     feats, rows, embed = tables.shape
     samp = arrival.shape[1]
     width = cross_weight.shape[2]
@@ -268,15 +280,16 @@
     wide = over_weight.shape[1]
     rblock = cotangent.shape[2]
     block = samp // ni
-    any_spec = pl.BlockSpec(memory_space=pl.ANY)
+    any_spec = pl.BlockSpec(memory_space=pltpu.HBM)
     vmem_spec = pl.BlockSpec(memory_space=pltpu.VMEM)
     over_out, grad = pl.pallas_call(
-        functools.partial(kernel, ni, nt),
+        functools.partial(kernel, ni, nt, groups),
         out_shape=(
             jax.ShapeDtypeStruct(cotangent.shape, BF16),
             jax.ShapeDtypeStruct((feats, ni, block, embed), BF16),
         ),
         in_specs=[any_spec] * 9,
+        name=name,
         out_specs=(vmem_spec, vmem_spec),
         scratch_shapes=[
             pltpu.VMEM((feats, 2, samp), jnp.int32),
@@ -311,9 +324,24 @@
             pltpu.SemaphoreType.DMA((4,)),
         ],
         compiler_params=pltpu.CompilerParams(
-            collective_id=0, has_side_effects=True, vmem_limit_bytes=60 * 1024 * 1024
+            collective_id=cid, has_side_effects=True, vmem_limit_bytes=vmem * 1024 * 1024
         ),
-    )(ids, arrival, tables, cross_weight, cross_bias, squeeze, over_weight, over_bias[None, :], cotangent)
+    )(
+        *(
+            pltpu.with_memory_space_constraint(x, pltpu.HBM)
+            for x in (
+                ids,
+                arrival,
+                tables,
+                cross_weight,
+                cross_bias,
+                squeeze,
+                over_weight,
+                over_bias[None, :],
+                cotangent,
+            )
+        )
+    )
     return over_out, grad.reshape(feats, samp, embed)
 
 

time: 99.7 us -> 90.7 us (0.910)
  Pallas kernels: 95.6 us -> 88.4 us
  local copies, waits for them, and re-layouts: 3.17 us -> 1.39 us
    pallas_call x1, Pallas kernels: 95.6 us -> 88.4 us  [local(): pl.pallas_call(functools.partial(kernel, ni, nt, groups), out_shape=(jax....]
    unnamed x2, local copies, waits for them, and re-layouts: 3.17 us -> 1.39 us
where the time goes in v2:
time: 90.7 us; the launch traced here: 90.5 us
  Pallas kernels  88.4 us (97%)
  local copies, waits for them, and re-layouts  1.39 us (2%)
    pallas_call x1, Pallas kernels, local(): pl.pallas_call(functools.partial(kernel, ni, nt, groups), out_shape=(jax....  88.4 us

profile of v2, /device:TPU:1, one launch (start us, length us, event | category | flops | bytes accessed | tf_op | source)
XLA Modules:
  0.0 90.5 jit_solution(16855583113008112007)
XLA Ops:
  0.6 88.4 %shard_map.104 = (bf16[1,1,8,512]{3,2,1,0:T(8,128)(2,1)S(1)}, bf16[8,32,8,128]{3,2,1,0:T(8,128)(2,1)S(1)}) custom-call(s32[8,2,256]{2,1,0:T(2,128)} %ids_hbm.1, s32[8,256]{1,0:T(8,128)} %arr_hbm.1, bf16[8,512,128]{2,1,0:T(8,128)(2,1)} %tab_hbm.1, bf16[1,2,1024,1024]{3,2,1,0:T(8,128)(2,1)} %cw_hbm.1, f32[1,2,1024]{2,1,0:T(2,128)} %cb_hbm.1, ...), custom_call_target="tpu_custom_call" | custom-call | tf_op jit(solution)/shard_map/pallas_call | solution.py:285
  89.1 0.6 copy.13
  89.7 0.8 copy.14

commit v3 on v2

--- a/solution.py
+++ b/solution.py
@@ -66,6 +66,9 @@
     own_sem,
     send_sem,
     recv_sem,
+    ring_sem,
+    over_sem,
+    mate_sem,
 ):
     feats, rows, embed = tab_ref.shape
     samp = arr_ref.shape[1]
@@ -77,7 +80,31 @@
     me_i = lax.axis_index("intra")
     me_t = lax.axis_index("tower")
 
+    zed, side = me_i // 2, lax.rem(me_i, 2)
+    ring = nt // 4
+    low, why, core = me_t // (2 * ring), lax.rem(me_t // 2, ring), lax.rem(me_t, 2)
+    cut = max(0, half // 4 - 1)
+
+    def at_i(dz, flip):
+        return lax.rem(zed + dz + half, half) * 2 + lax.rem(side + flip, 2)
+
+    def at_t(dy, flip_low, flip_core):
+        return (
+            lax.rem(low + flip_low, 2) * (2 * ring)
+            + lax.rem(why + dy + ring, ring) * 2
+            + lax.rem(core + flip_core, 2)
+        )
+
+    def signal(sem, axis, peer):
+        pl.semaphore_signal(sem, inc=1, device_id={axis: peer}, device_id_type=MESH)
+
     barrier = pltpu.get_barrier_semaphore()
+    greet = [("intra", at_i(0, 1)), ("intra", at_i(1, 0)), ("intra", at_i(-1, 0))]
+    greet += [("tower", at_t(0, 1, 0)), ("tower", at_t(0, 0, 1))]
+    if ring > 1:
+        greet += [("tower", at_t(1, 0, 0)), ("tower", at_t(-1, 0, 0))]
+    for axis, peer in greet:
+        signal(barrier, axis, peer)
 
     def peer_of(step, sets):
         each = half // sets
@@ -88,19 +115,6 @@
         z = lax.rem(me_i // 2 + base + sets * shift, half)
         xh = lax.rem(lax.rem(me_i, 2) + 1 - lax.rem(step, 2), 2)
         return z * 2 + xh
-
-    def greet_i(step, carry):
-        peer = peer_of(step, 1)
-        pl.semaphore_signal(barrier, inc=1, device_id={"intra": peer}, device_id_type=MESH)
-        return carry
-
-    def greet_t(step, carry):
-        peer = lax.rem(me_t + step, nt)
-        pl.semaphore_signal(barrier, inc=1, device_id={"tower": peer}, device_id_type=MESH)
-        return carry
-
-    lax.fori_loop(0, ni - 1, greet_i, 0)
-    lax.fori_loop(1, nt, greet_t, 0)
 
     loads = [
         pltpu.make_async_copy(src, dst, in_sem.at[at])
@@ -136,25 +150,45 @@
         pooled = dot(hot.astype(BF16), tab_ref[f])
         send1[:, f] = pooled.reshape(ni, block, embed).astype(BF16)
 
-    pl.semaphore_wait(barrier, ni + nt - 2)
-
-    def exchange_i(src, dst, at, sets):
+    pl.semaphore_wait(barrier, len(greet))
+
+    def send(src, dst, at, axis, peer, me):
+        pltpu.make_async_remote_copy(
+            src_ref=src(peer),
+            dst_ref=dst(me),
+            send_sem=send_sem.at[at],
+            recv_sem=recv_sem.at[at],
+            device_id={axis: peer},
+            device_id_type=MESH,
+        ).start()
+
+    def exchange_i(src, dst, at, sets, fresh):
         own = pltpu.make_async_copy(src(me_i), dst(me_i), own_sem.at[at])
         own.start()
+        if fresh:
+            for step in range(half // 2 + 1):
+                if step:
+                    signal(ring_sem.at[step - 1, 0], "intra", at_i(1, 0))
+                    signal(ring_sem.at[step - 1, 1], "intra", at_i(-1, 0))
+                    pl.semaphore_wait(ring_sem.at[step - 1, 0], 1)
+                    pl.semaphore_wait(ring_sem.at[step - 1, 1], 1)
+                for dist, flip in ((step + 1, 0), (step, 1)):
+                    if dist <= cut:
+                        send(src, dst, at, "intra", at_i(dist, flip), me_i)
+                        if dist:
+                            send(src, dst, at, "intra", at_i(-dist, flip), me_i)
 
         def start(step, carry):
             peer = peer_of(step, sets)
-
-            @pl.when(peer != me_i)
+            gap = lax.rem(peer // 2 - zed + half, half)
+            if fresh:
+                wanted = jnp.logical_and(gap > cut, gap < half - cut)
+            else:
+                wanted = peer != me_i
+
+            @pl.when(wanted)
             def _():
-                pltpu.make_async_remote_copy(
-                    src_ref=src(peer),
-                    dst_ref=dst(me_i),
-                    send_sem=send_sem.at[at],
-                    recv_sem=recv_sem.at[at],
-                    device_id={"intra": peer},
-                    device_id_type=MESH,
-                ).start()
+                send(src, dst, at, "intra", peer, me_i)
 
             return carry
 
@@ -166,21 +200,25 @@
         own.start()
 
         def start(step, carry):
-            peer = lax.rem(me_t + step, nt)
-            pltpu.make_async_remote_copy(
-                src_ref=src(peer),
-                dst_ref=dst(me_t),
-                send_sem=send_sem.at[at],
-                recv_sem=recv_sem.at[at],
-                device_id={"tower": peer},
-                device_id_type=MESH,
-            ).start()
+            k = step // 4
+            dy = ring // 2 + jnp.where(lax.rem(k, 2) == 1, -((k + 1) // 2), k // 2)
+            peer = at_t(dy, 1 - lax.rem(step // 2, 2), 1 - lax.rem(step, 2))
+            send(src, dst, at, "tower", peer, me_t)
             return carry
 
-        lax.fori_loop(1, nt, start, 0)
+        lax.fori_loop(0, nt - 1, start, 0)
         return own
 
-    own1 = exchange_i(lambda p: send1.at[p], lambda p: recv1.at[p], 0, groups)
+    own1 = exchange_i(lambda p: send1.at[p], lambda p: recv1.at[p], 0, groups, True)
+
+    signal(mate_sem, "tower", at_t(0, 0, 1))
+    pl.semaphore_wait(mate_sem, 1)
+    if ring > 1:
+        for step in range(ring // 2):
+            signal(over_sem.at[step, 0], "tower", at_t(1, 0, 0))
+            signal(over_sem.at[step, 1], "tower", at_t(-1, 0, 0))
+            pl.semaphore_wait(over_sem.at[step, 0], 1)
+            pl.semaphore_wait(over_sem.at[step, 1], 1)
 
     s_row = lax.broadcasted_iota(jnp.int32, (samp, samp), 0)
     s_col = lax.broadcasted_iota(jnp.int32, (samp, samp), 1)
@@ -261,7 +299,7 @@
         leaving = dot(perm_t[f], final[:, f * embed : (f + 1) * embed])
         send2[:, f] = leaving.reshape(ni, block, embed).astype(BF16)
 
-    own4 = exchange_i(lambda p: send2.at[p], lambda p: grad_ref.at[:, p], 3, 1)
+    own4 = exchange_i(lambda p: send2.at[p], lambda p: grad_ref.at[:, p], 3, 1, False)
     own4.wait()
     pltpu.make_async_copy(
         grad_ref.at[:, pl.ds(0, ni - 1)], grad_ref.at[:, pl.ds(0, ni - 1)], recv_sem.at[3]
@@ -322,6 +360,9 @@
             pltpu.SemaphoreType.DMA((4,)),
             pltpu.SemaphoreType.DMA((4,)),
             pltpu.SemaphoreType.DMA((4,)),
+            pltpu.SemaphoreType.REGULAR((ni // 4, 2)),
+            pltpu.SemaphoreType.REGULAR((max(1, nt // 8), 2)),
+            pltpu.SemaphoreType.REGULAR,
         ],
         compiler_params=pltpu.CompilerParams(
             collective_id=cid, has_side_effects=True, vmem_limit_bytes=vmem * 1024 * 1024

time: 90.7 us -> 94.9 us (1.046)
  Pallas kernels: 88.4 us -> 92.7 us
    pallas_call x1, Pallas kernels: 88.4 us -> 92.7 us  [local(): pl.pallas_call(functools.partial(kernel, ni, nt, groups), out_shape=(jax....]
where the time goes in v3:
time: 94.9 us; the launch traced here: 94.7 us
  Pallas kernels  92.7 us (98%)
  local copies, waits for them, and re-layouts  1.39 us (1%)
    pallas_call x1, Pallas kernels, local(): pl.pallas_call(functools.partial(kernel, ni, nt, groups), out_shape=(jax....  92.7 us

profile of v3, /device:TPU:1, one launch (start us, length us, event | category | flops | bytes accessed | tf_op | source)
XLA Modules:
  0.0 94.7 jit_solution(6452397572570760899)
XLA Ops:
  0.6 92.7 %shard_map.104 = (bf16[1,1,8,512]{3,2,1,0:T(8,128)(2,1)S(1)}, bf16[8,32,8,128]{3,2,1,0:T(8,128)(2,1)S(1)}) custom-call(s32[8,2,256]{2,1,0:T(2,128)} %ids_hbm.1, s32[8,256]{1,0:T(8,128)} %arr_hbm.1, bf16[8,512,128]{2,1,0:T(8,128)(2,1)} %tab_hbm.1, bf16[1,2,1024,1024]{3,2,1,0:T(8,128)(2,1)} %cw_hbm.1, f32[1,2,1024]{2,1,0:T(2,128)} %cb_hbm.1, ...), custom_call_target="tpu_custom_call" | custom-call | tf_op jit(solution)/shard_map/pallas_call | solution.py:323
  93.3 0.6 copy.13
  93.9 0.8 copy.14

commit v4 on v2

--- a/solution.py
+++ b/solution.py
@@ -77,31 +77,6 @@
     me_i = lax.axis_index("intra")
     me_t = lax.axis_index("tower")
 
-    barrier = pltpu.get_barrier_semaphore()
-
-    def peer_of(step, sets):
-        each = half // sets
-        k = lax.rem(step // 2, each)
-        near = -((k + 1) // 2)
-        shift = jnp.where(lax.rem(k, 2) == 1, near, k // 2) + each // 2
-        base = lax.rem((step // 2) // each + half - me_i // 2, sets)
-        z = lax.rem(me_i // 2 + base + sets * shift, half)
-        xh = lax.rem(lax.rem(me_i, 2) + 1 - lax.rem(step, 2), 2)
-        return z * 2 + xh
-
-    def greet_i(step, carry):
-        peer = peer_of(step, 1)
-        pl.semaphore_signal(barrier, inc=1, device_id={"intra": peer}, device_id_type=MESH)
-        return carry
-
-    def greet_t(step, carry):
-        peer = lax.rem(me_t + step, nt)
-        pl.semaphore_signal(barrier, inc=1, device_id={"tower": peer}, device_id_type=MESH)
-        return carry
-
-    lax.fori_loop(0, ni - 1, greet_i, 0)
-    lax.fori_loop(1, nt, greet_t, 0)
-
     loads = [
         pltpu.make_async_copy(src, dst, in_sem.at[at])
         for at, (src, dst) in enumerate(
@@ -118,7 +93,31 @@
             )
         )
     ]
-    for load in loads:
+    for load in loads[:3]:
+        load.start()
+
+    barrier = pltpu.get_barrier_semaphore()
+
+    def peer_of(step, sets):
+        each = half // sets
+        k = step // 2 % each
+        shift = (-((k + 1) // 2) if k % 2 else k // 2) + each // 2
+        base = lax.rem((step // 2) // each + half - me_i // 2, sets)
+        z = lax.rem(me_i // 2 + base + sets * shift, half)
+        xh = lax.rem(lax.rem(me_i, 2) + 1 - step % 2, 2)
+        return z * 2 + xh
+
+    def greet_t(step, carry):
+        peer = lax.rem(me_t + step, nt)
+        pl.semaphore_signal(barrier, inc=1, device_id={"tower": peer}, device_id_type=MESH)
+        return carry
+
+    for step in range(ni - 1):
+        peer = peer_of(step, 1)
+        pl.semaphore_signal(barrier, inc=1, device_id={"intra": peer}, device_id_type=MESH)
+    lax.fori_loop(1, nt, greet_t, 0)
+
+    for load in loads[3:]:
         load.start()
     loads[0].wait()
     loads[1].wait()
@@ -142,7 +141,7 @@
         own = pltpu.make_async_copy(src(me_i), dst(me_i), own_sem.at[at])
         own.start()
 
-        def start(step, carry):
+        def start(step):
             peer = peer_of(step, sets)
 
             @pl.when(peer != me_i)
@@ -156,17 +155,18 @@
                     device_id_type=MESH,
                 ).start()
 
-            return carry
-
-        lax.fori_loop(0, ni, start, 0)
+        for step in range(ni):
+            start(step)
         return own
 
     def exchange_t(src, dst, at):
         own = pltpu.make_async_copy(src(me_t), dst(me_t), own_sem.at[at])
         own.start()
 
-        def start(step, carry):
-            peer = lax.rem(me_t + step, nt)
+        ring = nt // 4
+        low, why, core = me_t // (2 * ring), lax.rem(me_t // 2, ring), lax.rem(me_t, 2)
+
+        def go(peer):
             pltpu.make_async_remote_copy(
                 src_ref=src(peer),
                 dst_ref=dst(me_t),
@@ -175,9 +175,17 @@
                 device_id={"tower": peer},
                 device_id_type=MESH,
             ).start()
-            return carry
-
-        lax.fori_loop(1, nt, start, 0)
+
+        def far(step):
+            k = step // 4
+            dy = ring // 2 + (-((k + 1) // 2) if k % 2 else k // 2)
+            flip_low, flip_core = 1 - step // 2 % 2, 1 - step % 2
+            return (
+                lax.rem(low + flip_low, 2) * (2 * ring) + lax.rem(why + dy, ring) * 2 + lax.rem(core + flip_core, 2)
+            )
+
+        for step in range(nt - 1):
+            go(far(step))
         return own
 
     own1 = exchange_i(lambda p: send1.at[p], lambda p: recv1.at[p], 0, groups)

time: 90.7 us -> 90 us (level)
  no operation moved by 1% of the time
where the time goes in v4:
time: 90 us; the launch traced here: 89.8 us
  Pallas kernels  87.8 us (98%)
  local copies, waits for them, and re-layouts  1.39 us (2%)
    pallas_call x1, Pallas kernels, local(): pl.pallas_call(functools.partial(kernel, ni, nt, groups), out_shape=(jax....  87.8 us

profile of v4, /device:TPU:1, one launch (start us, length us, event | category | flops | bytes accessed | tf_op | source)
XLA Modules:
  0.0 89.8 jit_solution(15403520269583731022)
XLA Ops:
  0.6 87.8 %shard_map.104 = (bf16[1,1,8,512]{3,2,1,0:T(8,128)(2,1)S(1)}, bf16[8,32,8,128]{3,2,1,0:T(8,128)(2,1)S(1)}) custom-call(s32[8,2,256]{2,1,0:T(2,128)} %ids_hbm.1, s32[8,256]{1,0:T(8,128)} %arr_hbm.1, bf16[8,512,128]{2,1,0:T(8,128)(2,1)} %tab_hbm.1, bf16[1,2,1024,1024]{3,2,1,0:T(8,128)(2,1)} %cw_hbm.1, f32[1,2,1024]{2,1,0:T(2,128)} %cb_hbm.1, ...), custom_call_target="tpu_custom_call" | custom-call | tf_op jit(solution)/shard_map/pallas_call | solution.py:293
  88.4 0.6 copy.13
  89.0 0.8 copy.14
